TPU v7x, 512 devices: a whole 4x4x16 slice. The times are simulated.
512 devices in a mesh: dp: 8 (over y, core), expert: 64 (over x, z).
Axes of the slice: x: 4, y: 4, z: 16, core: 2. Of those that a mesh axis runs over, the one named last changes fastest.
Arguments:
- layer_in: bfloat16 [2048, 4096], P('expert', 'dp'), may hold values from -6 to 6
- grad_out: bfloat16 [2048, 4096], P('expert', 'dp'), may hold values from -6 to 6
- gate_prob: float32 [2048, 8], P('expert'), may hold values from 0.05 to 0.6
- expert_ids: int32 [2048, 8], P('expert'), may hold values from 0 to 31, as said below
- replica_index: int32 [2048, 8], P('expert'), may hold values from 0 to 3, as said below
- slot_expert: int32 [64], replicated, may hold values from 0 to 31, as said below
- w_gate: bfloat16 [64, 4096, 1024], P('expert', None, 'dp')
- w_up: bfloat16 [64, 4096, 1024], P('expert', None, 'dp')
- w_down: bfloat16 [64, 1024, 4096], P('expert', 'dp')
Outputs:
- grad_in: bfloat16 [2048, 4096], P('expert', 'dp')
- grad_w_down: bfloat16 [64, 1024, 4096], P('expert', 'dp')
Inputs may be any that keep to these rules, and one draw needn't show every extreme that they name: `slot_expert`: every expert owns one run of consecutive slots, counted cyclically (slot 63 is followed by slot 0), of 1 to 4 slots; the runs cover all 64 slots. `expert_ids`: the 8 experts of one token are different. `replica_index`: each entry is below the number of slots of the expert of the same choice. Of the 32 tokens of one index of expert, at most 8 choices go to any one slot, and in every draw some slot receives exactly 8 from the tokens of every index of expert.
All inputs are finite; a program needn't handle non-finite values.
Results may differ from a plain program's by a relative error of at most 0.014.
Values may be sent and summed in bfloat16 or wider, within the bound.
No kernel may reach another device: no remote copies, remote signals or barrier semaphores. Data moves between devices by JAX's collectives and lax.ppermute only.
A program may use at most 64 MiB of HBM per device.

v0:
```python
import jax
import jax.numpy as jnp
from jax import lax
from jax.sharding import PartitionSpec as P

TOP = 8


def passed_along(value, axis, steps):
    count = lax.axis_size(axis)
    pairs = [(source, (source + steps) % count) for source in range(count)]
    return lax.ppermute(value, axis, pairs)


def body(
    layer_in, grad_out, gate_prob, expert_ids, replica_index, slot_expert, w_gate, w_up, w_down
):
    slots = lax.axis_size("expert")
    maxrep = min(4, slots // 8)
    tok_count = layer_in.shape[0]
    capacity = tok_count // maxrep
    recv_rows = slots * capacity
    expert_count = (8 - maxrep) * slots // 8
    slot_index = jnp.arange(slots, dtype=jnp.int32)
    expert_index = jnp.arange(expert_count, dtype=jnp.int32)
    is_start = slot_expert != jnp.roll(slot_expert, 1)
    first_slot = jnp.sum(
        jnp.where(
            (slot_expert[None, :] == expert_index[:, None]) & is_start[None, :],
            slot_index[None, :],
            0,
        ),
        axis=1,
    )
    own_index = lax.axis_index("expert")

    def route(ids, replicas):
        first = jnp.sum(jnp.where(ids[..., None] == expert_index, first_slot, 0), axis=-1)
        return (first + replicas) % slots

    codes = (expert_ids * 8 + replica_index).astype(jnp.float32)
    words = jnp.concatenate([codes, gate_prob], axis=1)
    all_words = lax.all_gather(words, "expert", axis=0, tiled=True)
    all_codes = all_words[:, :TOP].astype(jnp.int32)
    all_prob = all_words[:, TOP:]
    all_inputs = lax.all_gather(layer_in, "expert", axis=0, tiled=True)
    all_grads = lax.all_gather(grad_out, "expert", axis=0, tiled=True)
    here = route(all_codes // 8, all_codes % 8) == own_index
    prob_here = jnp.sum(jnp.where(here, all_prob, 0.0), axis=1)
    chosen = jnp.any(here, axis=1).astype(jnp.int32).reshape(slots, tok_count)
    rank = jnp.cumsum(chosen, axis=1) - chosen
    row = jnp.where(chosen > 0, slot_index[:, None] * capacity + rank, -1).reshape(-1)
    pick = (jnp.arange(recv_rows, dtype=jnp.int32)[:, None] == row[None, :]).astype(jnp.bfloat16)

    def picked(values):
        rows = jnp.dot(pick, values, preferred_element_type=jnp.float32).astype(jnp.bfloat16)
        return lax.all_gather(rows, "dp", axis=1, tiled=True)

    inputs = picked(all_inputs)
    scaled = picked((prob_here[:, None] * all_grads.astype(jnp.float32)).astype(jnp.bfloat16))
    width = inputs.shape[1]
    gate_matrix = w_gate[0]
    up_matrix = w_up[0]
    down_matrix = w_down[0]
    gate_pre = jnp.dot(inputs, gate_matrix, preferred_element_type=jnp.float32)
    up_pre = jnp.dot(inputs, up_matrix, preferred_element_type=jnp.float32)
    hidden = (jax.nn.silu(gate_pre) * up_pre).astype(jnp.bfloat16)
    contract_last = (((1,), (1,)), ((), ()))
    hidden_grad = lax.dot_general(
        scaled, down_matrix, contract_last, preferred_element_type=jnp.float32
    )
    sigma = jax.nn.sigmoid(gate_pre)
    gate_grad = (hidden_grad * up_pre * sigma * (1.0 + gate_pre * (1.0 - sigma))).astype(
        jnp.bfloat16
    )
    up_grad = (hidden_grad * gate_pre * sigma).astype(jnp.bfloat16)
    partial_value = lax.dot_general(
        gate_grad, gate_matrix, contract_last, preferred_element_type=jnp.float32
    )
    partial_value = partial_value + lax.dot_general(
        up_grad, up_matrix, contract_last, preferred_element_type=jnp.float32
    )
    partial_value = partial_value.reshape(slots, capacity, width)
    summed = lax.psum_scatter(
        partial_value.astype(jnp.bfloat16), "dp", scatter_dimension=2, tiled=True
    )
    returned = lax.all_to_all(summed, "expert", split_axis=0, concat_axis=0, tiled=True)
    flat_back = returned.reshape(recv_rows, -1)
    route_slot = route(expert_ids, replica_index)
    onehot = jnp.any(route_slot[:, :, None] == slot_index, axis=1).astype(jnp.int32)
    rank_back = jnp.cumsum(onehot, axis=0) - onehot
    place = jnp.arange(capacity, dtype=jnp.int32)
    unpick = ((onehot[:, :, None] > 0) & (rank_back[:, :, None] == place)).astype(jnp.bfloat16)
    grad_in = jnp.dot(
        unpick.reshape(tok_count, recv_rows), flat_back, preferred_element_type=jnp.float32
    ).astype(jnp.bfloat16)
    slot_partial = lax.dot_general(
        hidden, scaled, (((0,), (0,)), ((), ())), preferred_element_type=jnp.float32
    ).astype(jnp.bfloat16)
    expert_here = jnp.sum(jnp.where(slot_index == own_index, slot_expert, 0))

    def same_at(offset):
        neighbour = (own_index - offset) % slots
        match = jnp.any((slot_index == neighbour) & (slot_expert == expert_here))
        return match.astype(jnp.float32)

    own = slot_partial.astype(jnp.float32)
    left = own + same_at(1) * passed_along(slot_partial, "expert", 1).astype(jnp.float32)
    right = own + same_at(-1) * passed_along(slot_partial, "expert", -1).astype(jnp.float32)
    far_left = passed_along(left.astype(jnp.bfloat16), "expert", 2).astype(jnp.float32)
    far_right = passed_along(right.astype(jnp.bfloat16), "expert", -2).astype(jnp.float32)
    total = left + same_at(2) * far_left + (right - own) + same_at(-2) * far_right
    grad_w_down = total.astype(jnp.bfloat16)[None]
    return (grad_in, grad_w_down)


def solution(mesh):
    placed = (
        P("expert", "dp"),
        P("expert", "dp"),
        P("expert", None),
        P("expert", None),
        P("expert", None),
        P(),
        P("expert", None, "dp"),
        P("expert", None, "dp"),
        P("expert", "dp", None),
    )
    return jax.shard_map(
        body,
        mesh=mesh,
        in_specs=placed,
        out_specs=(P("expert", "dp"), P("expert", "dp", None)),
        check_vma=False,
    )
```

profile of v0, /device:TPU:6, one launch (start us, length us, event | category | flops | bytes accessed | tf_op | source)
XLA Modules:
  0.0 514.9 jit_solution(13106250262551552550)
XLA Ops:
  8.0 0.7 all-gather.6.cloned.1.call-update
  8.7 1.2 slice.14
  10.0 0.7 add_convert_fusion.1
  10.7 0.7 maximum_bitcast_fusion
  11.4 106.0 %all-gather = f32[64,32,16]{1,2,0:T(8,128)S(1)} all-gather(f32[1,32,16]{1,2,0:T(8,128)S(1)} %maximum_bitcast_fusion), channel_id=1, replica_groups=mesh['dp'=8,'expert'=64] {'expert'}, dimensions={0}, use_global_device_ids=true | all-gather | bytes 133120 | tf_op jit(solution)/shard_map/all_gather | solution.py:43
  118.4 1.4 broadcast_compare_fusion
  121.0 34.1 %all-gather.10.cloned.1.call-done = bf16[2048,512]{1,0:T(8,128)(2,1)} async-done(((bf16[32,512]{1,0:T(8,128)(2,1)}), bf16[2048,512]{1,0:T(8,128)(2,1)}) %all-gather.10.cloned.1.call-update) | async-done | bytes 2097168 | tf_op jit(solution)/shard_map/all_gather | solution.py:46
  155.1 3.6 fusion.12
  158.8 136.2 %all-gather.6.cloned.1.call-done = bf16[2048,512]{1,0:T(8,128)(2,1)} async-done(((bf16[32,512]{1,0:T(8,128)(2,1)}), bf16[2048,512]{1,0:T(8,128)(2,1)}) %all-gather.6.cloned.1.call-update) | async-done | bytes 2097168 | tf_op jit(solution)/shard_map/all_gather | solution.py:47
  295.1 3.8 fusion.11
  298.9 35.9 %all-gather.12.cloned.1.call-done = bf16[512,4096]{1,0:T(8,128)(2,1)} async-done(((bf16[512,512]{1,0:T(8,128)(2,1)}), bf16[512,4096]{1,0:T(8,128)(2,1)}) %all-gather.12.cloned.1.call-update) | async-done | bytes 4194320 | tf_op jit(solution)/shard_map/all_gather | solution.py:57
  334.9 3.6 fusion.16
  338.5 1.3 fusion.19
  339.7 37.0 %all-gather.8.cloned.1.call-done = bf16[512,4096]{1,0:T(8,128)(2,1)} async-done(((bf16[512,512]{1,0:T(8,128)(2,1)}), bf16[512,4096]{1,0:T(8,128)(2,1)}) %all-gather.8.cloned.1.call-update) | async-done | bytes 4194320 | tf_op jit(solution)/shard_map/all_gather | solution.py:57
  376.7 3.7 fusion.21
  380.4 1.3 fusion.14
  381.7 3.2 fusion
  384.9 3.0 convolution_convert_fusion
  387.9 3.5 collective-permute-start
  391.4 4.7 collective-permute-start.2
  396.1 0.7 and_reduce_fusion.2
  398.2 19.6 %collective-permute-done = bf16[128,4096]{1,0:T(8,128)(2,1)S(1)} collective-permute-done((bf16[128,4096]{1,0:T(8,128)(2,1)S(1)}, bf16[128,4096]{1,0:T(8,128)(2,1)S(1)}, u32[]{:S(2)}, u32[]{:S(2)}) %collective-permute-start) | collective-permute-done | bytes 1048608 | tf_op jit(solution)/shard_map/ppermute | solution.py:12
  417.7 1.2 collective-permute-done.2
  418.9 3.2 fusion.7
  422.1 5.2 %collective-permute-start.1 = (bf16[128,4096]{1,0:T(8,128)(2,1)}, bf16[128,4096]{1,0:T(8,128)(2,1)}, u32[]{:S(2)}, u32[]{:S(2)}) collective-permute-start(bf16[128,4096]{1,0:T(8,128)(2,1)} %get-tuple-element.10), channel_id=1, source_target_pairs={{0,2},{1,3},{2,4},{3,5},{4,6},{5,7},{6,8},{7,9},{8,10},{9,11},{10,... | collective-permute-start | bytes 3145736 | tf_op jit(solution)/shard_map/ppermute | solution.py:12
  427.3 3.7 collective-permute-start.3
  431.0 16.0 %all-to-all-start = ((bf16[64,8,512]{2,1,0:T(8,128)(2,1)}), bf16[64,8,512]{2,1,0:T(8,128)(2,1)}, u32[]{:S(2)}, u32[]{:S(2)}) async-start(bf16[64,8,512]{2,1,0:T(8,128)(2,1)} %reduce-scatter.2.cloned.1.call-done), calls=%async_computation.1 | async-start | bytes 1048576 | tf_op jit(solution)/shard_map/all_to_all | solution.py:87
  449.4 10.2 %collective-permute-done.1 = bf16[128,4096]{1,0:T(8,128)(2,1)} collective-permute-done((bf16[128,4096]{1,0:T(8,128)(2,1)}, bf16[128,4096]{1,0:T(8,128)(2,1)}, u32[]{:S(2)}, u32[]{:S(2)}) %collective-permute-start.1) | collective-permute-done | bytes 1048608 | tf_op jit(solution)/shard_map/ppermute | solution.py:12
  459.6 9.6 %collective-permute-done.3 = bf16[128,4096]{1,0:T(8,128)(2,1)} collective-permute-done((bf16[128,4096]{1,0:T(8,128)(2,1)}, bf16[128,4096]{1,0:T(8,128)(2,1)}, u32[]{:S(2)}, u32[]{:S(2)}) %collective-permute-start.3) | collective-permute-done | bytes 1048608 | tf_op jit(solution)/shard_map/ppermute | solution.py:12
  469.1 3.9 fusion.23
  473.0 33.4 %all-to-all-done = bf16[64,8,512]{2,1,0:T(8,128)(2,1)} async-done(((bf16[64,8,512]{2,1,0:T(8,128)(2,1)}), bf16[64,8,512]{2,1,0:T(8,128)(2,1)}, u32[]{:S(2)}, u32[]{:S(2)}) %all-to-all-start) | async-done | bytes 524320 | tf_op jit(solution)/shard_map/all_to_all | solution.py:87
  506.4 1.9 fusion.13
  (46 shorter events, 4.3 us)
Async XLA Ops:
  7.2 327.7 %copy-start = (bf16[1,4096,128]{2,1,0:T(8,128)(2,1)S(1)}, bf16[1,4096,128]{2,1,0:T(8,128)(2,1)}, u32[]{:S(2)}) copy-start(bf16[1,4096,128]{2,1,0:T(8,128)(2,1)} %param.15) | copy-start | bytes 3145732
  7.2 110.6 %copy-start.5 = (s32[64]{0:T(128)S(1)}, s32[64]{0:T(128)}, u32[]{:S(2)}) copy-start(s32[64]{0:T(128)} %param.14) | copy-start | bytes 772
  7.2 147.9 %all-gather.10.cloned.1.call-start = ((), (), s32[]{:S(2)}) async-start(), calls=%async_computation.4 | async-start | bytes 2129920 | tf_op jit(solution)/shard_map/all_gather | solution.py:46
  7.9 287.1 %all-gather.6.cloned.1.call-start = ((), (), s32[]{:S(2)}) async-start(), calls=%async_computation.2 | async-start | bytes 2129920 | tf_op jit(solution)/shard_map/all_gather | solution.py:47
  8.7 326.2 %all-gather.12.cloned.1.call-start = ((), (), s32[]{:S(2)}) async-start(), calls=%async_computation.5 | async-start | bytes 4718592 | tf_op jit(solution)/shard_map/all_gather | solution.py:57
  158.8 217.9 %all-gather.8.cloned.1.call-start = ((), (), s32[]{:S(2)}) async-start(), calls=%async_computation.3 | async-start | bytes 4718592 | tf_op jit(solution)/shard_map/all_gather | solution.py:57
  298.9 39.6 %copy-start.2 = (bf16[1,4096,128]{2,1,0:T(8,128)(2,1)S(1)}, bf16[1,4096,128]{2,1,0:T(8,128)(2,1)}, u32[]{:S(2)}) copy-start(bf16[1,4096,128]{2,1,0:T(8,128)(2,1)} %param.16) | copy-start | bytes 3145732
  298.9 132.1 %reduce-scatter.2.cloned.1.call-start = ((), (), s32[]{:S(2)}) async-start(), calls=%async_computation.6 | async-start | bytes 4718592 | tf_op jit(solution)/shard_map/reduce_scatter | solution.py:84
  334.9 3.6 copy-start.1
  387.9 29.8 %collective-permute-start = (bf16[128,4096]{1,0:T(8,128)(2,1)S(1)}, bf16[128,4096]{1,0:T(8,128)(2,1)S(1)}, u32[]{:S(2)}, u32[]{:S(2)}) collective-permute-start(bf16[128,4096]{1,0:T(8,128)(2,1)S(1)} %convolution_convert_fusion), channel_id=1, source_target_pairs={{0,1},{1,2},{2,3},{3,4},{4,5},{5,6},{6,7},{7,8},{8,9},{9,10},{10,1... | collective-permute-start | bytes 3145736 | tf_op jit(solution)/shard_map/ppermute | solution.py:12
  391.4 27.5 %collective-permute-start.2 = (bf16[128,4096]{1,0:T(8,128)(2,1)S(1)}, bf16[128,4096]{1,0:T(8,128)(2,1)}, u32[]{:S(2)}, u32[]{:S(2)}) collective-permute-start(bf16[128,4096]{1,0:T(8,128)(2,1)S(1)} %convolution_convert_fusion), channel_id=1, source_target_pairs={{0,63},{1,0},{2,1},{3,2},{4,3},{5,4},{6,5},{7,6},{8,7},{9,8},{10,9... | collective-permute-start | bytes 3145736 | tf_op jit(solution)/shard_map/ppermute | solution.py:12
  398.1 48.9 %copy-start.3 = (s32[32,8]{0,1:T(8,128)S(1)}, s32[32,8]{0,1:T(8,128)}, u32[]{:S(2)}) copy-start(s32[32,8]{0,1:T(8,128)} %param.12) | copy-start | bytes 3076
  398.2 48.9 %copy-start.4 = (s32[32,8]{0,1:T(8,128)S(1)}, s32[32,8]{0,1:T(8,128)}, u32[]{:S(2)}) copy-start(s32[32,8]{0,1:T(8,128)} %param.13) | copy-start | bytes 3076
  422.1 37.5 %collective-permute-start.1 = (bf16[128,4096]{1,0:T(8,128)(2,1)}, bf16[128,4096]{1,0:T(8,128)(2,1)}, u32[]{:S(2)}, u32[]{:S(2)}) collective-permute-start(bf16[128,4096]{1,0:T(8,128)(2,1)} %get-tuple-element.10), channel_id=1, source_target_pairs={{0,2},{1,3},{2,4},{3,5},{4,6},{5,7},{6,8},{7,9},{8,10},{9,11},{10,... | collective-permute-start | bytes 3145736 | tf_op jit(solution)/shard_map/ppermute | solution.py:12
  427.3 41.9 %collective-permute-start.3 = (bf16[128,4096]{1,0:T(8,128)(2,1)}, bf16[128,4096]{1,0:T(8,128)(2,1)}, u32[]{:S(2)}, u32[]{:S(2)}) collective-permute-start(bf16[128,4096]{1,0:T(8,128)(2,1)} %get-tuple-element.11), channel_id=1, source_target_pairs={{0,62},{1,63},{2,0},{3,1},{4,2},{5,3},{6,4},{7,5},{8,6},{9,7},{10,... | collective-permute-start | bytes 3145736 | tf_op jit(solution)/shard_map/ppermute | solution.py:12
  431.0 75.5 %all-to-all-start = ((bf16[64,8,512]{2,1,0:T(8,128)(2,1)}), bf16[64,8,512]{2,1,0:T(8,128)(2,1)}, u32[]{:S(2)}, u32[]{:S(2)}) async-start(bf16[64,8,512]{2,1,0:T(8,128)(2,1)} %reduce-scatter.2.cloned.1.call-done), calls=%async_computation.1 | async-start | bytes 1048576 | tf_op jit(solution)/shard_map/all_to_all | solution.py:87
Sparse Core Ops, SparseCore 0:
  11.0 144.1 all-gather.9
  158.1 136.9 all-gather.5
  297.8 37.0 all-gather.11
  336.8 39.8 all-gather.7
  385.1 45.8 reduce-scatter.1
where the time goes:
time: 516 us; the launch traced here: 515 us
  waiting for transfers between devices  319 us (62%)
  blocking collectives  106 us (21%)
  starting transfers between devices  33.2 us (6%)
  matrix products  25.4 us (5%)
  between operations  16.6 us (3%)
  other arithmetic  13 us (3%)
    all_gather x1, waiting for transfers between devices, body(): all_grads = lax.all_gather(grad_out, 'expert', axis=0, tiled=True)  136 us
    all_gather x1, blocking collectives, body(): all_words = lax.all_gather(words, 'expert', axis=0, tiled=True)  106 us
    all_gather x2, waiting for transfers between devices, picked(): return lax.all_gather(rows, 'dp', axis=1, tiled=True)  72.9 us
    ppermute x4, waiting for transfers between devices, passed_along(): return lax.ppermute(value, axis, pairs)  40.5 us
    all_gather x1, waiting for transfers between devices, body(): all_inputs = lax.all_gather(layer_in, 'expert', axis=0, tiled=True)  34.1 us
    all_to_all x1, waiting for transfers between devices, body(): lax.all_to_all(summed, 'expert', split_axis=0, concat_axis=0, tiled=True)  33.4 us
    ppermute x4, starting transfers between devices, passed_along(): return lax.ppermute(value, axis, pairs)  17 us
    all_to_all x1, starting transfers between devices, body(): lax.all_to_all(summed, 'expert', split_axis=0, concat_axis=0, tiled=True)  16 us
  transfers between devices with their start and end apart: 10, of which 9 were waited for; matrix products, arithmetic and copies ran while one was open for 6% of the time, Pallas kernels for 0%

commit v1 on v0

--- a/solution.py
+++ b/solution.py
@@ -4,6 +4,16 @@
 from jax.sharding import PartitionSpec as P
 
 TOP = 8
+
+
+def make_chunk_in(local_block, inp):
+    return jnp.split(
+        jax.lax.all_gather(
+            jnp.concatenate([local_block, inp], axis=1), "expert", axis=0, tiled=True
+        ),
+        [local_block.shape[1]],
+        axis=1,
+    )
 
 
 def passed_along(value, axis, steps):
@@ -43,8 +53,7 @@
     all_words = lax.all_gather(words, "expert", axis=0, tiled=True)
     all_codes = all_words[:, :TOP].astype(jnp.int32)
     all_prob = all_words[:, TOP:]
-    all_inputs = lax.all_gather(layer_in, "expert", axis=0, tiled=True)
-    all_grads = lax.all_gather(grad_out, "expert", axis=0, tiled=True)
+    all_inputs, all_grads = make_chunk_in(layer_in, inp=grad_out)
     here = route(all_codes // 8, all_codes % 8) == own_index
     prob_here = jnp.sum(jnp.where(here, all_prob, 0.0), axis=1)
     chosen = jnp.any(here, axis=1).astype(jnp.int32).reshape(slots, tok_count)

time: 516 us -> 382 us (0.74)
  waiting for transfers between devices: 319 us -> 183 us
    all_gather x2 -> x1, waiting for transfers between devices: 170 us -> 39.5 us  [make_chunk_in(): jax.lax.all_gather(jnp.concatenate([local_block, inp], axis=1), 'expert',...]
    all_to_all x1, waiting for transfers between devices: 33.4 us -> 20.7 us  [body(): lax.all_to_all(summed, 'expert', split_axis=0, concat_axis=0, tiled=True)]
    ppermute x4, waiting for transfers between devices: 40.5 us -> 53.1 us  [passed_along(): return lax.ppermute(value, axis, pairs)]
  transfers between devices with their start and end apart: 10 -> 9, of which waited for: 9 -> 8; matrix products, arithmetic and copies ran while one was open for 6% -> 7% of each run, Pallas kernels for 0% -> 0%
where the time goes in v1:
time: 382 us; the launch traced here: 381 us
  waiting for transfers between devices  183 us (48%)
  blocking collectives  106 us (28%)
  starting transfers between devices  33.4 us (9%)
  matrix products  25.4 us (7%)
  between operations  16.6 us (4%)
  other arithmetic  14.5 us (4%)
    all_gather x1, blocking collectives, body(): all_words = lax.all_gather(words, 'expert', axis=0, tiled=True)  106 us
    all_gather x2, waiting for transfers between devices, picked(): return lax.all_gather(rows, 'dp', axis=1, tiled=True)  69.8 us
    ppermute x4, waiting for transfers between devices, passed_along(): return lax.ppermute(value, axis, pairs)  53.1 us
    all_gather x1, waiting for transfers between devices, make_chunk_in(): jax.lax.all_gather(jnp.concatenate([local_block, inp], axis=1), 'expert',...  39.5 us
    all_to_all x1, waiting for transfers between devices, body(): lax.all_to_all(summed, 'expert', split_axis=0, concat_axis=0, tiled=True)  20.7 us
    ppermute x4, starting transfers between devices, passed_along(): return lax.ppermute(value, axis, pairs)  17.2 us
    all_to_all x1, starting transfers between devices, body(): lax.all_to_all(summed, 'expert', split_axis=0, concat_axis=0, tiled=True)  16 us
  transfers between devices with their start and end apart: 9, of which 8 were waited for; matrix products, arithmetic and copies ran while one was open for 7% of the time, Pallas kernels for 0%

profile of v1, /device:TPU:6, one launch (start us, length us, event | category | flops | bytes accessed | tf_op | source)
XLA Modules:
  0.0 381.0 jit_solution(16876403359934506211)
XLA Ops:
  7.2 1.5 pad_maximum_fusion
  8.8 1.2 slice.14
  10.0 0.7 add_convert_fusion.1
  10.8 0.7 maximum_bitcast_fusion
  11.4 105.9 %all-gather = f32[64,32,16]{1,2,0:T(8,128)S(1)} all-gather(f32[1,32,16]{1,2,0:T(8,128)S(1)} %maximum_bitcast_fusion), channel_id=1, replica_groups=mesh['dp'=8,'expert'=64] {'expert'}, dimensions={0}, use_global_device_ids=true | all-gather | bytes 133120 | tf_op jit(solution)/shard_map/all_gather | solution.py:53
  118.4 1.3 broadcast_compare_fusion
  121.0 39.5 %all-gather.5.cloned.1.call-done = bf16[2048,1024]{1,0:T(8,128)(2,1)} async-done(((bf16[32,1024]{1,0:T(8,128)(2,1)}), bf16[2048,1024]{1,0:T(8,128)(2,1)}) %all-gather.5.cloned.1.call-update) | async-done | bytes 4194320 | tf_op jit(solution)/shard_map/all_gather | solution.py:11
  160.6 3.6 fusion.14
  164.3 3.8 fusion.13
  168.1 32.7 %all-gather.9.cloned.1.call-done = bf16[512,4096]{1,0:T(8,128)(2,1)} async-done(((bf16[512,512]{1,0:T(8,128)(2,1)}), bf16[512,4096]{1,0:T(8,128)(2,1)}) %all-gather.9.cloned.1.call-update) | async-done | bytes 4194320 | tf_op jit(solution)/shard_map/all_gather | solution.py:66
  200.8 3.6 fusion.20
  204.4 1.3 fusion.23
  205.7 37.1 %all-gather.7.cloned.1.call-done = bf16[512,4096]{1,0:T(8,128)(2,1)} async-done(((bf16[512,512]{1,0:T(8,128)(2,1)}), bf16[512,4096]{1,0:T(8,128)(2,1)}) %all-gather.7.cloned.1.call-update) | async-done | bytes 4194320 | tf_op jit(solution)/shard_map/all_gather | solution.py:66
  242.8 3.7 fusion.25
  246.6 1.3 fusion.18
  247.8 3.2 fusion
  251.1 3.0 convolution_convert_fusion
  254.0 3.5 collective-permute-start
  257.5 4.9 %collective-permute-start.2 = (bf16[128,4096]{1,0:T(8,128)(2,1)S(1)}, bf16[128,4096]{1,0:T(8,128)(2,1)}, u32[]{:S(2)}, u32[]{:S(2)}) collective-permute-start(bf16[128,4096]{1,0:T(8,128)(2,1)S(1)} %convolution_convert_fusion), channel_id=1, source_target_pairs={{0,63},{1,0},{2,1},{3,2},{4,3},{5,4},{6,5},{7,6},{8,7},{9,8},{10,9... | collective-permute-start | bytes 3145736 | tf_op jit(solution)/shard_map/ppermute | solution.py:22
  262.4 0.7 and_reduce_fusion.2
  264.5 19.4 %collective-permute-done = bf16[128,4096]{1,0:T(8,128)(2,1)S(1)} collective-permute-done((bf16[128,4096]{1,0:T(8,128)(2,1)S(1)}, bf16[128,4096]{1,0:T(8,128)(2,1)S(1)}, u32[]{:S(2)}, u32[]{:S(2)}) %collective-permute-start) | collective-permute-done | bytes 1048608 | tf_op jit(solution)/shard_map/ppermute | solution.py:22
  283.8 1.2 collective-permute-done.2
  285.0 3.2 fusion.9
  288.2 5.0 %collective-permute-start.1 = (bf16[128,4096]{1,0:T(8,128)(2,1)}, bf16[128,4096]{1,0:T(8,128)(2,1)}, u32[]{:S(2)}, u32[]{:S(2)}) collective-permute-start(bf16[128,4096]{1,0:T(8,128)(2,1)} %get-tuple-element.10), channel_id=1, source_target_pairs={{0,2},{1,3},{2,4},{3,5},{4,6},{5,7},{6,8},{7,9},{8,10},{9,11},{10,... | collective-permute-start | bytes 3145736 | tf_op jit(solution)/shard_map/ppermute | solution.py:22
  293.2 3.9 %collective-permute-start.3 = (bf16[128,4096]{1,0:T(8,128)(2,1)}, bf16[128,4096]{1,0:T(8,128)(2,1)}, u32[]{:S(2)}, u32[]{:S(2)}) collective-permute-start(bf16[128,4096]{1,0:T(8,128)(2,1)} %get-tuple-element.11), channel_id=1, source_target_pairs={{0,62},{1,63},{2,0},{3,1},{4,2},{5,3},{6,4},{7,5},{8,6},{9,7},{10,... | collective-permute-start | bytes 3145736 | tf_op jit(solution)/shard_map/ppermute | solution.py:22
  297.1 16.0 %all-to-all-start = ((bf16[64,8,512]{2,1,0:T(8,128)(2,1)}), bf16[64,8,512]{2,1,0:T(8,128)(2,1)}, u32[]{:S(2)}, u32[]{:S(2)}) async-start(bf16[64,8,512]{2,1,0:T(8,128)(2,1)} %reduce-scatter.2.cloned.1.call-done), calls=%async_computation.1 | async-start | bytes 1048576 | tf_op jit(solution)/shard_map/all_to_all | solution.py:96
  314.6 0.7 select_reduce_fusion.1
  315.5 9.9 %collective-permute-done.1 = bf16[128,4096]{1,0:T(8,128)(2,1)} collective-permute-done((bf16[128,4096]{1,0:T(8,128)(2,1)}, bf16[128,4096]{1,0:T(8,128)(2,1)}, u32[]{:S(2)}, u32[]{:S(2)}) %collective-permute-start.1) | collective-permute-done | bytes 1048608 | tf_op jit(solution)/shard_map/ppermute | solution.py:22
  325.4 22.6 %collective-permute-done.3 = bf16[128,4096]{1,0:T(8,128)(2,1)} collective-permute-done((bf16[128,4096]{1,0:T(8,128)(2,1)}, bf16[128,4096]{1,0:T(8,128)(2,1)}, u32[]{:S(2)}, u32[]{:S(2)}) %collective-permute-start.3) | collective-permute-done | bytes 1048608 | tf_op jit(solution)/shard_map/ppermute | solution.py:22
  348.0 3.9 %fusion.27 = bf16[1,128,4096]{2,1,0:T(8,128)(2,1)} fusion(bf16[128,4096]{1,0:T(8,128)(2,1)} %collective-permute-done.3, f32[]{:T(128)S(6)} %convert_element_type.129, bf16[128,4096]{1,0:T(8,128)(2,1)} %collective-permute-done.2, f32[]{:T(128)S(6)} %convert_element_type.127, bf16[128,4096]{1,0:T(8,128)(2,1)} %collective-permute-done.1, ...), kind=kLoop, calls=%fused_computation.35 | loop fusion | flops 8388608 | bytes 6291472 | tf_op jit(solution)/shard_map/broadcast_in_dim | solution.py:122
  351.9 20.7 %all-to-all-done = bf16[64,8,512]{2,1,0:T(8,128)(2,1)} async-done(((bf16[64,8,512]{2,1,0:T(8,128)(2,1)}), bf16[64,8,512]{2,1,0:T(8,128)(2,1)}, u32[]{:S(2)}, u32[]{:S(2)}) %all-to-all-start) | async-done | bytes 524320 | tf_op jit(solution)/shard_map/all_to_all | solution.py:96
  372.5 1.9 fusion.17
  (44 shorter events, 2.9 us)
Async XLA Ops:
  7.2 193.7 %copy-start = (bf16[1,4096,128]{2,1,0:T(8,128)(2,1)S(1)}, bf16[1,4096,128]{2,1,0:T(8,128)(2,1)}, u32[]{:S(2)}) copy-start(bf16[1,4096,128]{2,1,0:T(8,128)(2,1)} %param.15) | copy-start | bytes 3145732
  7.2 110.6 %copy-start.5 = (s32[64]{0:T(128)S(1)}, s32[64]{0:T(128)}, u32[]{:S(2)}) copy-start(s32[64]{0:T(128)} %param.14) | copy-start | bytes 772
  7.2 153.4 %all-gather.5.cloned.1.call-start = ((), (), s32[]{:S(2)}) async-start(), calls=%async_computation.2 | async-start | bytes 4259840 | tf_op jit(solution)/shard_map/all_gather | solution.py:11
  8.7 192.1 %all-gather.9.cloned.1.call-start = ((), (), s32[]{:S(2)}) async-start(), calls=%async_computation.4 | async-start | bytes 4718592 | tf_op jit(solution)/shard_map/all_gather | solution.py:66
  164.2 78.6 %all-gather.7.cloned.1.call-start = ((), (), s32[]{:S(2)}) async-start(), calls=%async_computation.3 | async-start | bytes 4718592 | tf_op jit(solution)/shard_map/all_gather | solution.py:66
  168.1 36.3 %copy-start.2 = (bf16[1,4096,128]{2,1,0:T(8,128)(2,1)S(1)}, bf16[1,4096,128]{2,1,0:T(8,128)(2,1)}, u32[]{:S(2)}) copy-start(bf16[1,4096,128]{2,1,0:T(8,128)(2,1)} %param.16) | copy-start | bytes 3145732
  168.1 129.0 %reduce-scatter.2.cloned.1.call-start = ((), (), s32[]{:S(2)}) async-start(), calls=%async_computation.5 | async-start | bytes 4718592 | tf_op jit(solution)/shard_map/reduce_scatter | solution.py:93
  200.8 3.6 copy-start.1
  254.0 29.8 %collective-permute-start = (bf16[128,4096]{1,0:T(8,128)(2,1)S(1)}, bf16[128,4096]{1,0:T(8,128)(2,1)S(1)}, u32[]{:S(2)}, u32[]{:S(2)}) collective-permute-start(bf16[128,4096]{1,0:T(8,128)(2,1)S(1)} %convolution_convert_fusion), channel_id=1, source_target_pairs={{0,1},{1,2},{2,3},{3,4},{4,5},{5,6},{6,7},{7,8},{8,9},{9,10},{10,1... | collective-permute-start | bytes 3145736 | tf_op jit(solution)/shard_map/ppermute | solution.py:22
  257.5 27.5 %collective-permute-start.2 = (bf16[128,4096]{1,0:T(8,128)(2,1)S(1)}, bf16[128,4096]{1,0:T(8,128)(2,1)}, u32[]{:S(2)}, u32[]{:S(2)}) collective-permute-start(bf16[128,4096]{1,0:T(8,128)(2,1)S(1)} %convolution_convert_fusion), channel_id=1, source_target_pairs={{0,63},{1,0},{2,1},{3,2},{4,3},{5,4},{6,5},{7,6},{8,7},{9,8},{10,9... | collective-permute-start | bytes 3145736 | tf_op jit(solution)/shard_map/ppermute | solution.py:22
  264.4 48.7 %copy-start.3 = (s32[32,8]{0,1:T(8,128)S(1)}, s32[32,8]{0,1:T(8,128)}, u32[]{:S(2)}) copy-start(s32[32,8]{0,1:T(8,128)} %param.12) | copy-start | bytes 3076
  264.4 48.8 %copy-start.4 = (s32[32,8]{0,1:T(8,128)S(1)}, s32[32,8]{0,1:T(8,128)}, u32[]{:S(2)}) copy-start(s32[32,8]{0,1:T(8,128)} %param.13) | copy-start | bytes 3076
  288.2 37.2 %collective-permute-start.1 = (bf16[128,4096]{1,0:T(8,128)(2,1)}, bf16[128,4096]{1,0:T(8,128)(2,1)}, u32[]{:S(2)}, u32[]{:S(2)}) collective-permute-start(bf16[128,4096]{1,0:T(8,128)(2,1)} %get-tuple-element.10), channel_id=1, source_target_pairs={{0,2},{1,3},{2,4},{3,5},{4,6},{5,7},{6,8},{7,9},{8,10},{9,11},{10,... | collective-permute-start | bytes 3145736 | tf_op jit(solution)/shard_map/ppermute | solution.py:22
  293.2 54.8 %collective-permute-start.3 = (bf16[128,4096]{1,0:T(8,128)(2,1)}, bf16[128,4096]{1,0:T(8,128)(2,1)}, u32[]{:S(2)}, u32[]{:S(2)}) collective-permute-start(bf16[128,4096]{1,0:T(8,128)(2,1)} %get-tuple-element.11), channel_id=1, source_target_pairs={{0,62},{1,63},{2,0},{3,1},{4,2},{5,3},{6,4},{7,5},{8,6},{9,7},{10,... | collective-permute-start | bytes 3145736 | tf_op jit(solution)/shard_map/ppermute | solution.py:22
  297.1 75.4 %all-to-all-start = ((bf16[64,8,512]{2,1,0:T(8,128)(2,1)}), bf16[64,8,512]{2,1,0:T(8,128)(2,1)}, u32[]{:S(2)}, u32[]{:S(2)}) async-start(bf16[64,8,512]{2,1,0:T(8,128)(2,1)} %reduce-scatter.2.cloned.1.call-done), calls=%async_computation.1 | async-start | bytes 1048576 | tf_op jit(solution)/shard_map/all_to_all | solution.py:96
Sparse Core Ops, SparseCore 0:
  11.5 148.9 all-gather.4
  164.4 36.4 all-gather.8
  202.9 39.8 all-gather.6
  251.2 45.8 reduce-scatter.1
